TPU v7x, 512 devices: a whole 4x4x16 slice. The times are simulated.
512 devices in a mesh: net: 16 (over z), seg: 8 (over y, core), corner: 4 (over x).
Axes of the slice: x: 4, y: 4, z: 16, core: 2. Of those that a mesh axis runs over, the one named last changes fastest.
Arguments:
- tile_values: bfloat16 [8192, 128, 1024], P(('net', 'seg', 'corner')), may hold values from -48 to 48
- tile_coords: int32 [8192, 3], P(('net', 'seg', 'corner')), may hold values from 0 to 511, as said below
- tile_count: int32 [512], P(('net', 'seg', 'corner')), may hold values from 12 to 16, as said below
- owner_map: int32 [512], P('net'), may hold values from 0 to 511, as said below
- corner_factor: bfloat16 [64, 256], P('corner')
- seg_factor: bfloat16 [65536, 256], P(('seg', 'net'))
Outputs:
- net_factor: float32 [65536, 256], P(('net', 'seg', 'corner'))
Inputs may be any that keep to these rules, and one draw needn't show every extreme that they name: `tile_coords`: row t of device d gives a corner block within the corner range stored by d's corner index, a net block that owner_map assigns to an owner slot of d's net index, and a segment block within the segment range of d's seg index. Among a device's 16 rows at most 2 name segment blocks stored by any one device of the net axis, and on every device two live rows name segment blocks stored by the same device of the net axis. The first tile_count[d] rows of device d are live; the others are ignored. `owner_map`: A permutation of the 512 net blocks.
All inputs are finite; a program needn't handle non-finite values.
Results may differ from a plain program's by a relative error of at most 0.0058.
The roundings to bfloat16 on the way count: a program that leaves them out, or rounds other values in their place, can miss the bound.
Values may be sent and summed in bfloat16 or wider, within the bound.
No kernel may reach another device: no remote copies, remote signals or barrier semaphores. Data moves between devices by JAX's collectives and lax.ppermute only.
A program may use at most 64 MiB of HBM per device.

v0:
```python
import jax
import jax.numpy as jnp
from jax import lax
from jax.sharding import PartitionSpec as P

CBLK = 8
GRP = 4


def solve_rows(gram, mttkrp):
    cholesky_low = jnp.linalg.cholesky(gram)
    forward = lax.linalg.triangular_solve(cholesky_low, mttkrp.T, left_side=True, lower=True)
    backward = lax.linalg.triangular_solve(
        cholesky_low, forward, left_side=True, lower=True, transpose_a=True
    )
    return backward.T


def contract(packed):
    values, corner_rows, seg_rows = packed
    khatri = (
        corner_rows.astype(jnp.float32)[:, :, None, :] * seg_rows.astype(jnp.float32)[:, None, :, :]
    ).astype(jnp.bfloat16)
    khatri = khatri.reshape(values.shape[0], values.shape[2], corner_rows.shape[2])
    return jnp.einsum("tnj,tjr->tnr", values, khatri, preferred_element_type=jnp.float32)


def body(tile_values, tile_coords, tile_count, owner_map, corner_factor, seg_factor):
    slot_total = tile_values.shape[0]
    net_rows = tile_values.shape[1]
    columns = corner_factor.shape[1]
    seg_width = tile_values.shape[2] // CBLK
    held_blocks = seg_factor.shape[0] // seg_width
    net_devices = lax.axis_size("net")
    corner_local = tile_coords[:, 0] - lax.axis_index("corner") * (corner_factor.shape[0] // CBLK)
    seg_local = tile_coords[:, 2] - lax.axis_index("seg") * (held_blocks * net_devices)
    corner_sel = jnp.take(corner_factor.reshape(-1, CBLK, columns), corner_local, axis=0)
    gathered = lax.all_gather(seg_factor, "net", axis=0, tiled=True)
    seg_sel = jnp.take(gathered.reshape(-1, seg_width, columns), seg_local, axis=0)
    groups = slot_total // GRP
    partial_value = lax.map(
        contract,
        (
            tile_values.reshape(groups, GRP, net_rows, -1),
            corner_sel.reshape(groups, GRP, CBLK, columns),
            seg_sel.reshape(groups, GRP, seg_width, columns),
        ),
    )
    partial_value = partial_value.reshape(slot_total, net_rows * columns)
    live_mask = jnp.arange(slot_total, dtype=jnp.int32) < tile_count[0]
    member = ((tile_coords[:, 1][:, None] == owner_map[None, :]) & live_mask[:, None]).astype(
        jnp.float32
    )
    summed = jnp.dot(
        member.T, partial_value, precision=lax.Precision.HIGHEST, preferred_element_type=jnp.float32
    )
    mttkrp = lax.psum_scatter(
        summed.reshape(net_rows * lax.axis_size(("seg", "corner")), columns),
        ("seg", "corner"),
        scatter_dimension=0,
        tiled=True,
    )
    corner_part = jnp.dot(corner_factor.T, corner_factor, preferred_element_type=jnp.float32)
    seg_part = jnp.dot(seg_factor.T, seg_factor, preferred_element_type=jnp.float32)
    seg_gram = lax.psum(seg_part, ("net", "seg"))
    corner_gram = lax.psum(corner_part, "corner")
    return solve_rows(corner_gram * seg_gram, mttkrp)


def solution(mesh):
    return jax.shard_map(
        body,
        mesh=mesh,
        in_specs=(
            P(("net", "seg", "corner"), None, None),
            P(("net", "seg", "corner"), None),
            P(("net", "seg", "corner")),
            P("net"),
            P("corner", None),
            P(("seg", "net"), None),
        ),
        out_specs=P(("net", "seg", "corner"), None),
        check_vma=False,
    )
```

profile of v0, /device:TPU:8, one launch (start us, length us, event | category | flops | bytes accessed | tf_op | source)
XLA Modules:
  0.0 481.0 jit_solution(18225845388589294858)
XLA Ops:
  8.1 2.1 fusion.23
  10.3 1.0 fusion.22
  14.3 79.2 %all-gather.2.cloned.1.call-done = bf16[8192,256]{1,0:T(8,128)(2,1)} async-done(((bf16[512,256]{1,0:T(8,128)(2,1)}), bf16[8192,256]{1,0:T(8,128)(2,1)}) %all-gather.2.cloned.1.call-update) | async-done | bytes 4194320 | tf_op jit(solution)/shard_map/all_gather | solution.py:38
  93.5 2.8 gather_fusion.1
  96.5 12.6 %while.11 = (s32[]{:T(128)}, f32[4,4,128,256]{3,2,1,0:T(8,128)}, bf16[4,4,128,1024]{3,2,1,0:T(8,128)(2,1)}, bf16[4,4,8,256]{3,2,1,0:T(8,128)(2,1)S(1)}, bf16[4,4,128,256]{3,2,1,0:T(8,128)(2,1)S(1)}, /*index=5*/s32[]{:T(128)}) while((s32[]{:T(128)}, f32[4,4,128,256]{3,2,1,0:T(8,128)}, bf16[4,4,128,1024]{3,2,1,0:T(8,128)(2,1)}, ...), condition=%wide.region_7.8_spmd, body=%wide.region_6.7_spmd.sunk | while | flops 270671872 | bytes 7160917 | solution.py:41
  97.2 2.5 fusion.43
  100.3 2.5 fusion.43
  103.5 2.5 fusion.43
  106.6 2.5 fusion.43
  109.1 2.8 copy.13
  111.9 3.5 fusion.15
  115.5 4.9 %reshape.80 = f32[4096,256]{1,0:T(8,128)} reshape(f32[32,32768]{1,0:T(8,128)} %fusion.15) | data formatting | bytes 8388608 | tf_op jit(solution)/shard_map/reshape | solution.py:58
  120.4 232.0 %all-reduce.6.cloned.1.call-done = f32[256,256]{0,1:T(8,128)} async-done(((f32[256,256]{0,1:T(8,128)}), f32[256,256]{0,1:T(8,128)}) %all-reduce.6.cloned.1.call-update) | async-done | bytes 262160 | tf_op jit(solution)/shard_map/psum | solution.py:65
  352.4 56.2 %all-reduce.4.cloned.1.call-done = f32[256,256]{0,1:T(8,128)} async-done(((f32[256,256]{0,1:T(8,128)}), f32[256,256]{0,1:T(8,128)}) %all-reduce.4.cloned.1.call-update) | async-done | bytes 262160 | tf_op jit(solution)/shard_map/psum | solution.py:66
  408.6 1.1 mul.24
  409.8 11.7 %cholesky.50 = f32[128,128]{1,0:T(8,128)S(1)} custom-call(f32[128,128]{1,0:T(8,128)S(1)} %cholesky.118), custom_call_target="Cholesky" | custom-call | tf_op jit(solution)/shard_map/jit(cholesky)/cholesky | solution.py:11
  421.6 9.8 %custom-call.16 = f32[1,128,128]{1,2,0:T(8,128)S(1)} custom-call(f32[1,128,128]{2,1,0:T(8,128)S(1)} %get-tuple-element.68), custom_call_target="InvertDiagBlocksLowerTriangular" | custom-call | tf_op jit(solution)/shard_map/jit(cholesky)/cholesky | solution.py:11
  431.9 11.7 %cholesky.105 = f32[128,128]{1,0:T(8,128)S(1)} custom-call(f32[128,128]{1,0:T(8,128)S(1)} %convolution_subtract_fusion.2), custom_call_target="Cholesky" | custom-call | tf_op jit(solution)/shard_map/jit(cholesky)/cholesky | solution.py:11
  445.7 3.9 while.12
  446.3 1.3 bitcast_dynamic-update-slice_fusion.2
  448.3 1.3 bitcast_dynamic-update-slice_fusion.2
  449.6 19.9 %custom-call.17 = f32[2,128,128]{1,2,0:T(8,128)S(1)} custom-call(f32[2,128,128]{2,1,0:T(8,128)S(1)} %get-tuple-element.40), custom_call_target="InvertDiagBlocksLowerTriangular" | custom-call | tf_op jit(solution)/shard_map/triangular_solve | solution.py:13
  469.5 1.1 fusion.5
  470.7 1.1 convolution_subtract_fusion.1
  (59 shorter events, 10.4 us)
Async XLA Ops:
  7.4 2.9 copy-start
  7.4 86.2 %all-gather.2.cloned.1.call-start = ((), (), s32[]{:S(2)}) async-start(), calls=%async_computation.3 | async-start | bytes 4456448 | tf_op jit(solution)/shard_map/all_gather | solution.py:38
  8.1 344.3 %all-reduce.6.cloned.1.call-start = ((), (), s32[]{:S(2)}) async-start(), calls=%async_computation.2 | async-start | bytes 524288 | tf_op jit(solution)/shard_map/psum | solution.py:65
  10.3 398.3 %all-reduce.4.cloned.1.call-start = ((), (), s32[]{:S(2)}) async-start(), calls=%async_computation.1 | async-start | bytes 524288 | tf_op jit(solution)/shard_map/psum | solution.py:66
  11.3 458.2 %reduce-scatter.2.cloned.1.call-start = ((), (), s32[]{:S(2)}) async-start(), calls=%async_computation.4 | async-start | bytes 4325376 | tf_op jit(solution)/shard_map/reduce_scatter | solution.py:57
  109.1 2.8 copy-start.1
Sparse Core Ops, SparseCore 0:
  10.3 83.2 all-gather.1
  120.5 101.2 reduce-scatter.1
Sparse Core Ops, SparseCore 1:
  12.4 339.9 all-reduce.5
  354.7 53.8 all-reduce.3
where the time goes:
time: 482 us; the launch traced here: 481 us
  waiting for transfers between devices  368 us (76%)
  other arithmetic  58.6 us (12%)
  matrix products  20.2 us (4%)
  between operations  17 us (4%)
  local copies, waits for them, and re-layouts  16.8 us (3%)
    psum x1, waiting for transfers between devices, body(): seg_gram = lax.psum(seg_part, ('net', 'seg'))  232 us
    all_gather x1, waiting for transfers between devices, body(): gathered = lax.all_gather(seg_factor, 'net', axis=0, tiled=True)  79.2 us
    psum x1, waiting for transfers between devices, body(): corner_gram = lax.psum(corner_part, 'corner')  56.2 us
    another operation x6, other arithmetic, solve_rows(): cholesky_low = jnp.linalg.cholesky(gram)  34 us
    another operation x3, other arithmetic, solve_rows(): lax.linalg.triangular_solve(cholesky_low, forward, left_side=True, lower=...  19.9 us
    dot_general x4, matrix products, contract(): jnp.einsum('tnj,tjr->tnr', values, khatri, preferred_element_type=jnp.flo...  9.96 us
  transfers between devices with their start and end apart: 4, of which 3 were waited for; matrix products, arithmetic and copies ran while one was open for 19% of the time, Pallas kernels for 0%

commit v1 on v0

--- a/solution.py
+++ b/solution.py
@@ -63,7 +63,11 @@
     corner_part = jnp.dot(corner_factor.T, corner_factor, preferred_element_type=jnp.float32)
     seg_part = jnp.dot(seg_factor.T, seg_factor, preferred_element_type=jnp.float32)
     seg_gram = lax.psum(seg_part, ("net", "seg"))
-    corner_gram = lax.psum(corner_part, "corner")
+    corner_gram = corner_part
+    for hop in (1, 2):
+        corner_gram = corner_gram + lax.ppermute(
+            corner_gram, "corner", [(dev, dev ^ hop) for dev in range(4)]
+        )
     return solve_rows(corner_gram * seg_gram, mttkrp)
 
 

time: 482 us -> 426 us (0.88)
  the two profiles are of different devices: /device:TPU:8 before, /device:TPU:1 now
where the time goes in v1:
time: 426 us; the launch traced here: 425 us
  waiting for transfers between devices  305 us (72%)
  other arithmetic  58.3 us (14%)
  matrix products  19.5 us (5%)
  between operations  17 us (4%)
  local copies, waits for them, and re-layouts  16.8 us (4%)
  starting transfers between devices  8.11 us (2%)
    psum x1, waiting for transfers between devices, body(): seg_gram = lax.psum(seg_part, ('net', 'seg'))  227 us
    all_gather x1, waiting for transfers between devices, body(): gathered = lax.all_gather(seg_factor, 'net', axis=0, tiled=True)  73 us
    another operation x6, other arithmetic, solve_rows(): cholesky_low = jnp.linalg.cholesky(gram)  34 us
    another operation x3, other arithmetic, solve_rows(): lax.linalg.triangular_solve(cholesky_low, forward, left_side=True, lower=...  19.7 us
    dot_general x4, matrix products, contract(): jnp.einsum('tnj,tjr->tnr', values, khatri, preferred_element_type=jnp.flo...  9.96 us
  transfers between devices with their start and end apart: 5, of which 3 were waited for; matrix products, arithmetic and copies ran while one was open for 21% of the time, Pallas kernels for 0%

profile of v1, /device:TPU:1, one launch (start us, length us, event | category | flops | bytes accessed | tf_op | source)
XLA Modules:
  0.0 425.0 jit_solution(18317328971682359909)
XLA Ops:
  8.1 2.1 fusion.23
  13.3 73.0 %all-gather.2.cloned.1.call-done = bf16[8192,256]{1,0:T(8,128)(2,1)} async-done(((bf16[512,256]{1,0:T(8,128)(2,1)}), bf16[8192,256]{1,0:T(8,128)(2,1)}) %all-gather.2.cloned.1.call-update) | async-done | bytes 4194320 | tf_op jit(solution)/shard_map/all_gather | solution.py:38
  86.3 2.8 gather_fusion.1
  89.3 12.6 %while.11 = (s32[]{:T(128)}, f32[4,4,128,256]{3,2,1,0:T(8,128)}, bf16[4,4,128,1024]{3,2,1,0:T(8,128)(2,1)}, bf16[4,4,8,256]{3,2,1,0:T(8,128)(2,1)S(1)}, bf16[4,4,128,256]{3,2,1,0:T(8,128)(2,1)S(1)}, /*index=5*/s32[]{:T(128)}) while((s32[]{:T(128)}, f32[4,4,128,256]{3,2,1,0:T(8,128)}, bf16[4,4,128,1024]{3,2,1,0:T(8,128)(2,1)}, ...), condition=%wide.region_6.7_spmd, body=%wide.region_5.6_spmd.sunk | while | flops 270671872 | bytes 7160917 | solution.py:41
  89.9 2.5 fusion.43
  93.1 2.5 fusion.43
  96.2 2.5 fusion.43
  99.3 2.5 fusion.43
  101.8 2.8 copy.14
  104.7 3.5 fusion.15
  108.2 4.9 %reshape.80 = f32[4096,256]{1,0:T(8,128)} reshape(f32[32,32768]{1,0:T(8,128)} %fusion.15) | data formatting | bytes 8388608 | tf_op jit(solution)/shard_map/reshape | solution.py:58
  113.4 3.2 collective-permute-start
  116.5 4.3 %collective-permute-done = f32[256,256]{0,1:T(8,128)S(1)} collective-permute-done((f32[256,256]{0,1:T(8,128)S(1)}, f32[256,256]{0,1:T(8,128)S(1)}, u32[]{:S(2)}, u32[]{:S(2)}) %collective-permute-start) | collective-permute-done | bytes 262176 | tf_op jit(solution)/shard_map/ppermute | solution.py:68
  120.9 4.9 %collective-permute-start.1 = (f32[256,256]{0,1:T(8,128)S(1)}, f32[256,256]{0,1:T(8,128)S(1)}, u32[]{:S(2)}, u32[]{:S(2)}) collective-permute-start(f32[256,256]{0,1:T(8,128)S(1)} %add.49), channel_id=1, source_target_pairs={{0,2},{1,3},{2,0},{3,1},{4,6},{5,7},{6,4},{7,5},{8,10},{9,11},{10,... | collective-permute-start | bytes 786440 | tf_op jit(solution)/shard_map/ppermute | solution.py:68
  125.8 226.8 %all-reduce.3.cloned.1.call-done = f32[256,256]{0,1:T(8,128)} async-done(((f32[256,256]{0,1:T(8,128)}), f32[256,256]{0,1:T(8,128)}) %all-reduce.3.cloned.1.call-update) | async-done | bytes 262160 | tf_op jit(solution)/shard_map/psum | solution.py:65
  353.8 11.7 %cholesky.50 = f32[128,128]{1,0:T(8,128)S(1)} custom-call(f32[128,128]{1,0:T(8,128)S(1)} %cholesky.118), custom_call_target="Cholesky" | custom-call | tf_op jit(solution)/shard_map/jit(cholesky)/cholesky | solution.py:11
  365.6 9.8 %custom-call.16 = f32[1,128,128]{1,2,0:T(8,128)S(1)} custom-call(f32[1,128,128]{2,1,0:T(8,128)S(1)} %get-tuple-element.68), custom_call_target="InvertDiagBlocksLowerTriangular" | custom-call | tf_op jit(solution)/shard_map/jit(cholesky)/cholesky | solution.py:11
  375.9 11.7 %cholesky.105 = f32[128,128]{1,0:T(8,128)S(1)} custom-call(f32[128,128]{1,0:T(8,128)S(1)} %convolution_subtract_fusion.2), custom_call_target="Cholesky" | custom-call | tf_op jit(solution)/shard_map/jit(cholesky)/cholesky | solution.py:11
  389.7 4.1 while.12
  390.5 1.3 bitcast_dynamic-update-slice_fusion.2
  392.4 1.3 bitcast_dynamic-update-slice_fusion.2
  393.8 19.7 %custom-call.17 = f32[2,128,128]{1,2,0:T(8,128)S(1)} custom-call(f32[2,128,128]{2,1,0:T(8,128)S(1)} %get-tuple-element.40), custom_call_target="InvertDiagBlocksLowerTriangular" | custom-call | tf_op jit(solution)/shard_map/triangular_solve | solution.py:13
  413.5 1.1 fusion.5
  414.6 1.1 convolution_subtract_fusion.1
  (61 shorter events, 11.6 us)
Async XLA Ops:
  7.4 5.3 %copy-start = (bf16[16,256]{1,0:T(8,128)(2,1)S(1)}, bf16[16,256]{1,0:T(8,128)(2,1)}, u32[]{:S(2)}) copy-start(bf16[16,256]{1,0:T(8,128)(2,1)} %param.12) | copy-start | bytes 24580
  7.4 78.9 %all-gather.2.cloned.1.call-start = ((), (), s32[]{:S(2)}) async-start(), calls=%async_computation.2 | async-start | bytes 4456448 | tf_op jit(solution)/shard_map/all_gather | solution.py:38
  8.1 344.5 %all-reduce.3.cloned.1.call-start = ((), (), s32[]{:S(2)}) async-start(), calls=%async_computation.1 | async-start | bytes 524288 | tf_op jit(solution)/shard_map/psum | solution.py:65
  10.2 403.2 %reduce-scatter.2.cloned.1.call-start = ((), (), s32[]{:S(2)}) async-start(), calls=%async_computation.3 | async-start | bytes 4325376 | tf_op jit(solution)/shard_map/reduce_scatter | solution.py:57
  101.8 2.8 copy-start.1
  113.4 7.5 %collective-permute-start = (f32[256,256]{0,1:T(8,128)S(1)}, f32[256,256]{0,1:T(8,128)S(1)}, u32[]{:S(2)}, u32[]{:S(2)}) collective-permute-start(f32[256,256]{0,1:T(8,128)S(1)} %fusion.22), channel_id=1, source_target_pairs={{0,1},{1,0},{2,3},{3,2},{4,5},{5,4},{6,7},{7,6},{8,9},{9,8},{10,11... | collective-permute-start | bytes 786440 | tf_op jit(solution)/shard_map/ppermute | solution.py:68
  120.9 231.7 %collective-permute-start.1 = (f32[256,256]{0,1:T(8,128)S(1)}, f32[256,256]{0,1:T(8,128)S(1)}, u32[]{:S(2)}, u32[]{:S(2)}) collective-permute-start(f32[256,256]{0,1:T(8,128)S(1)} %add.49), channel_id=1, source_target_pairs={{0,2},{1,3},{2,0},{3,1},{4,6},{5,7},{6,4},{7,5},{8,10},{9,11},{10,... | collective-permute-start | bytes 786440 | tf_op jit(solution)/shard_map/ppermute | solution.py:68
Sparse Core Ops, SparseCore 0:
  10.3 75.9 all-gather.1
  113.2 108.0 reduce-scatter.1
Sparse Core Ops, SparseCore 1:
  12.4 340.1 all-reduce.2

commit v2 on v0

--- a/solution.py
+++ b/solution.py
@@ -35,7 +35,9 @@
     corner_local = tile_coords[:, 0] - lax.axis_index("corner") * (corner_factor.shape[0] // CBLK)
     seg_local = tile_coords[:, 2] - lax.axis_index("seg") * (held_blocks * net_devices)
     corner_sel = jnp.take(corner_factor.reshape(-1, CBLK, columns), corner_local, axis=0)
-    gathered = lax.all_gather(seg_factor, "net", axis=0, tiled=True)
+    gathered = jnp.concatenate(
+        lax.all_to_all(jnp.stack([seg_factor] * lax.axis_size("net")), "net", 0, 0), axis=0
+    )
     seg_sel = jnp.take(gathered.reshape(-1, seg_width, columns), seg_local, axis=0)
     groups = slot_total // GRP
     partial_value = lax.map(

time: 482 us -> 559 us (1.16)
  waiting for transfers between devices: 368 us -> 429 us
  starting transfers between devices: 0.13 us -> 15.5 us
    all_to_all x0 -> x1, waiting for transfers between devices: none -> 180 us  [body(): lax.all_to_all(jnp.stack([seg_factor] * lax.axis_size('net')), 'net', 0, 0)]
    all_gather x1 -> x0, waiting for transfers between devices: 79.2 us -> none  [body(): gathered = lax.all_gather(seg_factor, 'net', axis=0, tiled=True)]
    psum x1, waiting for transfers between devices: 232 us -> 193 us  [body(): seg_gram = lax.psum(seg_part, ('net', 'seg'))]
    all_to_all x0 -> x1, starting transfers between devices: none -> 15.4 us  [body(): lax.all_to_all(jnp.stack([seg_factor] * lax.axis_size('net')), 'net', 0, 0)]
  transfers between devices with their start and end apart: 4 -> 4, of which waited for: 3 -> 3; matrix products, arithmetic and copies ran while one was open for 19% -> 16% of each run, Pallas kernels for 0% -> 0%
where the time goes in v2:
time: 559 us
  waiting for transfers between devices  429 us (77%)
  other arithmetic  57.8 us (10%)
  local copies, waits for them, and re-layouts  19.4 us (3%)
  matrix products  19.2 us (3%)
  between operations  17 us (3%)
  starting transfers between devices  15.5 us (3%)
    psum x1, waiting for transfers between devices, body(): seg_gram = lax.psum(seg_part, ('net', 'seg'))  193 us
    all_to_all x1, waiting for transfers between devices, body(): lax.all_to_all(jnp.stack([seg_factor] * lax.axis_size('net')), 'net', 0, 0)  180 us
    psum x1, waiting for transfers between devices, body(): corner_gram = lax.psum(corner_part, 'corner')  56.5 us
    another operation x6, other arithmetic, solve_rows(): cholesky_low = jnp.linalg.cholesky(gram)  34 us
    another operation x3, other arithmetic, solve_rows(): lax.linalg.triangular_solve(cholesky_low, forward, left_side=True, lower=...  19.9 us
    all_to_all x1, starting transfers between devices, body(): lax.all_to_all(jnp.stack([seg_factor] * lax.axis_size('net')), 'net', 0, 0)  15.4 us
  transfers between devices with their start and end apart: 4, of which 3 were waited for; matrix products, arithmetic and copies ran while one was open for 16% of the time, Pallas kernels for 0%

profile of v2, /device:TPU:8, one launch (start us, length us, event | category | flops | bytes accessed | tf_op | source)
XLA Modules:
  0.0 558.6 jit_solution(3753553670603413467)
XLA Ops:
  7.4 3.3 stack.2
  10.7 15.4 %all-to-all-start = ((bf16[16,512,256]{2,1,0:T(8,128)(2,1)}), bf16[16,512,256]{2,1,0:T(8,128)(2,1)}, u32[]{:S(2)}, u32[]{:S(2)}) async-start(bf16[16,512,256]{2,1,0:T(8,128)(2,1)} %stack.2), calls=%async_computation | async-start | bytes 8388608 | tf_op jit(solution)/shard_map/all_to_all | solution.py:39
  29.8 179.9 %all-to-all-done = bf16[16,512,256]{2,1,0:T(8,128)(2,1)} async-done(((bf16[16,512,256]{2,1,0:T(8,128)(2,1)}), bf16[16,512,256]{2,1,0:T(8,128)(2,1)}, u32[]{:S(2)}, u32[]{:S(2)}) %all-to-all-start) | async-done | bytes 4194336 | tf_op jit(solution)/shard_map/all_to_all | solution.py:39
  209.7 2.8 gather_fusion.1
  212.7 12.6 %while.11 = (s32[]{:T(128)}, f32[4,4,128,256]{3,2,1,0:T(8,128)}, bf16[4,4,128,1024]{3,2,1,0:T(8,128)(2,1)}, bf16[4,4,8,256]{3,2,1,0:T(8,128)(2,1)S(1)}, bf16[4,4,128,256]{3,2,1,0:T(8,128)(2,1)S(1)}, /*index=5*/s32[]{:T(128)}) while((s32[]{:T(128)}, f32[4,4,128,256]{3,2,1,0:T(8,128)}, bf16[4,4,128,1024]{3,2,1,0:T(8,128)(2,1)}, ...), condition=%wide.region_7.8_spmd, body=%wide.region_6.7_spmd.sunk | while | flops 270671872 | bytes 7160909 | solution.py:43
  213.4 2.5 fusion.43
  216.6 2.5 fusion.43
  219.7 2.5 fusion.43
  222.9 2.5 fusion.43
  225.3 2.8 copy.13
  228.2 3.5 fusion.15
  231.7 4.9 reshape.78
  236.6 193.0 %all-reduce.6.cloned.1.call-done = f32[256,256]{0,1:T(8,128)} async-done(((f32[256,256]{0,1:T(8,128)}), f32[256,256]{0,1:T(8,128)}) %all-reduce.6.cloned.1.call-update) | async-done | bytes 262160 | tf_op jit(solution)/shard_map/psum | solution.py:67
  429.6 56.5 %all-reduce.4.cloned.1.call-done = f32[256,256]{0,1:T(8,128)} async-done(((f32[256,256]{0,1:T(8,128)}), f32[256,256]{0,1:T(8,128)}) %all-reduce.4.cloned.1.call-update) | async-done | bytes 262160 | tf_op jit(solution)/shard_map/psum | solution.py:68
  486.1 1.1 mul.24
  487.4 11.7 %cholesky.50 = f32[128,128]{1,0:T(8,128)S(1)} custom-call(f32[128,128]{1,0:T(8,128)S(1)} %cholesky.118), custom_call_target="Cholesky" | custom-call | tf_op jit(solution)/shard_map/jit(cholesky)/cholesky | solution.py:11
  499.1 9.8 %custom-call.16 = f32[1,128,128]{1,2,0:T(8,128)S(1)} custom-call(f32[1,128,128]{2,1,0:T(8,128)S(1)} %get-tuple-element.68), custom_call_target="InvertDiagBlocksLowerTriangular" | custom-call | tf_op jit(solution)/shard_map/jit(cholesky)/cholesky | solution.py:11
  509.5 11.7 %cholesky.105 = f32[128,128]{1,0:T(8,128)S(1)} custom-call(f32[128,128]{1,0:T(8,128)S(1)} %convolution_subtract_fusion.2), custom_call_target="Cholesky" | custom-call | tf_op jit(solution)/shard_map/jit(cholesky)/cholesky | solution.py:11
  523.2 3.9 while.12
  523.9 1.3 bitcast_dynamic-update-slice_fusion.2
  525.8 1.3 bitcast_dynamic-update-slice_fusion.2
  527.1 19.9 %custom-call.17 = f32[2,128,128]{1,2,0:T(8,128)S(1)} custom-call(f32[2,128,128]{2,1,0:T(8,128)S(1)} %get-tuple-element.40), custom_call_target="InvertDiagBlocksLowerTriangular" | custom-call | tf_op jit(solution)/shard_map/triangular_solve | solution.py:13
  547.1 1.1 fusion.5
  548.2 1.1 convolution_subtract_fusion.1
  (63 shorter events, 10.2 us)
Async XLA Ops:
  7.4 19.9 %copy-start = (bf16[16,256]{1,0:T(8,128)(2,1)S(1)}, bf16[16,256]{1,0:T(8,128)(2,1)}, u32[]{:S(2)}) copy-start(bf16[16,256]{1,0:T(8,128)(2,1)} %param.12) | copy-start | bytes 24580
  10.7 15.4 %copy-start.1 = (bf16[512,256]{1,0:T(8,128)(2,1)S(1)}, bf16[512,256]{1,0:T(8,128)(2,1)}, u32[]{:S(2)}) copy-start(bf16[512,256]{1,0:T(8,128)(2,1)} %param.13) | copy-start | bytes 786436
  10.7 17.5 %copy-start.3 = (s32[16,3]{0,1:T(4,128)S(1)}, s32[16,3]{0,1:T(4,128)}, u32[]{:S(2)}) copy-start(s32[16,3]{0,1:T(4,128)} %param.9) | copy-start | bytes 580
  10.7 199.0 %all-to-all-start = ((bf16[16,512,256]{2,1,0:T(8,128)(2,1)}), bf16[16,512,256]{2,1,0:T(8,128)(2,1)}, u32[]{:S(2)}, u32[]{:S(2)}) async-start(bf16[16,512,256]{2,1,0:T(8,128)(2,1)} %stack.2), calls=%async_computation | async-start | bytes 8388608 | tf_op jit(solution)/shard_map/all_to_all | solution.py:39
  26.1 403.5 %all-reduce.6.cloned.1.call-start = ((), (), s32[]{:S(2)}) async-start(), calls=%async_computation.3 | async-start | bytes 524288 | tf_op jit(solution)/shard_map/psum | solution.py:67
  27.2 459.0 %all-reduce.4.cloned.1.call-start = ((), (), s32[]{:S(2)}) async-start(), calls=%async_computation.2 | async-start | bytes 524288 | tf_op jit(solution)/shard_map/psum | solution.py:68
  28.2 518.9 %reduce-scatter.2.cloned.1.call-start = ((), (), s32[]{:S(2)}) async-start(), calls=%async_computation.4 | async-start | bytes 4325376 | tf_op jit(solution)/shard_map/reduce_scatter | solution.py:59
  225.3 2.8 copy-start.2
Sparse Core Ops, SparseCore 0:
  30.8 398.8 all-reduce.5
  432.1 54.0 all-reduce.3
Sparse Core Ops, SparseCore 1:
  236.7 104.5 reduce-scatter.1
